TPU v7x, 32 devices: a whole 2x2x4 slice. The times are simulated.
32 devices in a mesh: ctx: 8 (over z, y), fsdp: 4 (over x, core).
Axes of the slice: x: 2, y: 2, z: 4, core: 2. Of those that a mesh axis runs over, the one named last changes fastest.
Arguments:
- tokens: bfloat16 [4, 4096, 1024], P('fsdp', 'ctx'), may hold values from -6 to 6
- block_pos: int32 [4, 16], P('fsdp'), may hold values from 0 to 15, each once within a row
- gain_attn: bfloat16 [1024], P('fsdp'), may hold values from 0.25 to 1.75
- w_query: bfloat16 [1024, 256], P('fsdp'), may hold values from -0.1875 to 0.1875
- w_key: bfloat16 [1024, 256], P('fsdp'), may hold values from -0.1875 to 0.1875
- w_value: bfloat16 [1024, 1024], P('fsdp'), may hold values from -0.1875 to 0.1875
- w_out: bfloat16 [1024, 1024], P('fsdp'), may hold values from -2 to 2
- gain_ffn: bfloat16 [1024], P('fsdp'), may hold values from 0.25 to 1.75
- w_gate: bfloat16 [1024, 2752], P('fsdp'), may hold values from -0.1875 to 0.1875
- w_up: bfloat16 [1024, 2752], P('fsdp'), may hold values from -0.1875 to 0.1875
- w_down: bfloat16 [2752, 1024], P('fsdp'), may hold values from -0.109375 to 0.109375
- cotangent: bfloat16 [4, 4096, 1024], P('fsdp', 'ctx'), may hold values from -6 to 6
Outputs:
- output: bfloat16 [4, 4096, 1024], P('fsdp', 'ctx')
- grad_tokens: float32 [4, 4096, 1024], P('fsdp', 'ctx')
- grad_gain_attn: float32 [1024], P('fsdp')
- grad_query: float32 [1024, 256], P('fsdp')
- grad_key: float32 [1024, 256], P('fsdp')
- grad_value: float32 [1024, 1024], P('fsdp')
- grad_out: float32 [1024, 1024], P('fsdp')
- grad_gain_ffn: float32 [1024], P('fsdp')
- grad_gate: float32 [1024, 2752], P('fsdp')
- grad_up: float32 [1024, 2752], P('fsdp')
- grad_down: float32 [2752, 1024], P('fsdp')
Inputs may be any that keep to these rules, and one draw needn't show every extreme that they name: `block_pos`: each row is a permutation of the 16 position blocks of one sequence.
All inputs are finite; a program needn't handle non-finite values.
Results may differ from a plain program's by a relative error of at most 0.015.
Values may be sent and summed in bfloat16 or wider, within the bound.
A program may use at most 512 MiB of HBM per device.

v0:
```python
import jax
import jax.numpy as jnp
from jax import lax
from jax.sharding import PartitionSpec as P

HEADS = 16
FDIM = 16
VDIM = 64
BLOCK = 256
highest = lax.Precision.HIGHEST
eps_norm = 1e-05
root_half = 0.7071067811865476


def features(scaled):
    outer_prod = scaled[..., :, None] * scaled[..., None, :]
    flattened = (
        outer_prod.reshape(scaled.shape[:-1] + (scaled.shape[-1] * scaled.shape[-1],)) * root_half
    )
    constant = jnp.ones(scaled.shape[:-1] + (1,), jnp.float32)
    return jnp.concatenate([constant, scaled, flattened], axis=-1)


def features_back(scaled, grad_feat):
    feat_dim = scaled.shape[-1]
    linear = grad_feat[..., 1 : 1 + feat_dim]
    square = (
        grad_feat[..., 1 + feat_dim :].reshape(scaled.shape[:-1] + (feat_dim, feat_dim)) * root_half
    )
    return linear + jnp.einsum("...ab,...b->...a", square + jnp.swapaxes(square, -1, -2), scaled)


def norm_forward(values, gain_vector):
    inv_rms = lax.rsqrt(jnp.mean(values * values, axis=-1, keepdims=True) + eps_norm)
    return (values * inv_rms * gain_vector, inv_rms)


def norm_backward(values, inv_rms, gain_vector, grad_normed):
    weighted = grad_normed * gain_vector
    grad_gain = jnp.sum(grad_normed * values * inv_rms, axis=0)
    grad_values = inv_rms * weighted - values * (inv_rms * inv_rms * inv_rms) * jnp.mean(
        weighted * values, axis=-1, keepdims=True
    )
    return (grad_values, grad_gain)


def block_group():
    for group_size in (8, 4, 2):
        return group_size
    return 1


def body(
    tokens,
    block_pos,
    gain_attn,
    w_query,
    w_key,
    w_value,
    w_out,
    gain_ffn,
    w_gate,
    w_up,
    w_down,
    cotangent,
):
    gathered = (
        lax.all_gather(gain_attn, "fsdp", axis=0, tiled=True),
        lax.all_gather(w_query, "fsdp", axis=0, tiled=True),
        lax.all_gather(w_key, "fsdp", axis=0, tiled=True),
        lax.all_gather(w_value, "fsdp", axis=0, tiled=True),
        lax.all_gather(w_out, "fsdp", axis=0, tiled=True),
        lax.all_gather(gain_ffn, "fsdp", axis=0, tiled=True),
        lax.all_gather(w_gate, "fsdp", axis=0, tiled=True),
        lax.all_gather(w_up, "fsdp", axis=0, tiled=True),
        lax.all_gather(w_down, "fsdp", axis=0, tiled=True),
    )
    norm_one_gain = gathered[0].astype(jnp.float32)
    query_full, key_full, value_full, out_full = (
        gathered[1],
        gathered[2],
        gathered[3],
        gathered[4],
    )
    norm_two_gain = gathered[5].astype(jnp.float32)
    gate_full, up_full, down_full = (gathered[6], gathered[7], gathered[8])
    residual = tokens[0].astype(jnp.float32)
    row_count = residual.shape[0]
    local_blocks = row_count // BLOCK
    feat_width = 1 + FDIM + FDIM * FDIM
    positions = block_pos[0]
    own_positions = lax.dynamic_slice_in_dim(
        positions, lax.axis_index("ctx") * local_blocks, local_blocks
    )
    normed_one, inv_rms_one = norm_forward(residual, norm_one_gain)
    normed_one_low = normed_one.astype(jnp.bfloat16)
    queries = jnp.dot(normed_one_low, query_full, preferred_element_type=jnp.float32).astype(
        jnp.bfloat16
    )
    keys_all = jnp.dot(normed_one_low, key_full, preferred_element_type=jnp.float32).astype(
        jnp.bfloat16
    )
    values_all = jnp.dot(normed_one_low, value_full, preferred_element_type=jnp.float32).astype(
        jnp.bfloat16
    )
    query_blocks = queries.reshape(local_blocks, BLOCK, HEADS, FDIM)
    key_blocks = keys_all.reshape(local_blocks, BLOCK, HEADS, FDIM)
    value_blocks = values_all.reshape(local_blocks, BLOCK, HEADS, VDIM)
    query_scaled = query_blocks.astype(jnp.float32) * 0.5
    key_scaled = key_blocks.astype(jnp.float32) * 0.5
    phi_query = features(query_scaled).astype(jnp.bfloat16)
    phi_key = features(key_scaled).astype(jnp.bfloat16)
    state_zero = jnp.zeros((local_blocks, HEADS, feat_width, VDIM), jnp.float32)
    norm_zero = jnp.zeros((local_blocks, HEADS, feat_width), jnp.float32)
    running = (state_zero, norm_zero)
    key_piece = lax.all_gather(keys_all, "ctx", axis=0, tiled=True)
    value_piece = lax.all_gather(values_all, "ctx", axis=0, tiled=True)
    block_count = key_piece.shape[0] // BLOCK
    group_size = block_group()
    others = positions
    key_groups = key_piece.reshape(block_count // group_size, group_size, BLOCK, HEADS, FDIM)
    value_groups = value_piece.reshape(block_count // group_size, group_size, BLOCK, HEADS, VDIM)
    other_groups = others.reshape(block_count // group_size, group_size)

    def one_group(inner_sum, group_args):
        keys_here, values_here, places = group_args
        key_feat = features(keys_here.astype(jnp.float32) * 0.5).astype(jnp.bfloat16)
        states = jnp.einsum(
            "gthf,gthv->ghfv", key_feat, values_here, preferred_element_type=jnp.float32
        )
        norm_sums = jnp.sum(key_feat.astype(jnp.float32), axis=1)
        earlier = (places[None, :] < own_positions[:, None]).astype(jnp.float32)
        return (
            (
                inner_sum[0] + jnp.einsum("ig,ghfv->ihfv", earlier, states, precision=highest),
                inner_sum[1] + jnp.einsum("ig,ghf->ihf", earlier, norm_sums, precision=highest),
            ),
            None,
        )

    running, unused = lax.scan(one_group, running, (key_groups, value_groups, other_groups))
    prefix, prefix_norm = running
    phi_query_wide = phi_query.astype(jnp.float32)
    scores = (
        jnp.einsum("nshf,nthf->nhst", query_blocks, key_blocks, preferred_element_type=jnp.float32)
        * 0.25
    )
    kernel = 1.0 + scores + 0.5 * scores * scores
    kernel_low = kernel.astype(jnp.bfloat16)
    numerator = jnp.einsum(
        "nhst,nthv->nshv", kernel_low, value_blocks, preferred_element_type=jnp.float32
    ) + jnp.einsum("nshf,nhfv->nshv", phi_query_wide, prefix, precision=highest)
    denominator = jnp.transpose(jnp.sum(kernel, axis=-1), (0, 2, 1)) + jnp.einsum(
        "nshf,nhf->nsh", phi_query_wide, prefix_norm, precision=highest
    )
    attention_full = numerator / denominator[..., None]
    attention_low = attention_full.reshape(row_count, HEADS * VDIM).astype(jnp.bfloat16)
    middle = residual + jnp.dot(attention_low, out_full, preferred_element_type=jnp.float32)
    normed_two, inv_rms_two = norm_forward(middle, norm_two_gain)
    normed_two_low = normed_two.astype(jnp.bfloat16)
    gate_pre = jnp.dot(normed_two_low, gate_full, preferred_element_type=jnp.float32)
    up_pre = jnp.dot(normed_two_low, up_full, preferred_element_type=jnp.float32)
    sigmoid_gate = jax.nn.sigmoid(gate_pre)
    silu_gate = gate_pre * sigmoid_gate
    hidden_low = (silu_gate * up_pre).astype(jnp.bfloat16)
    result = middle + jnp.dot(hidden_low, down_full, preferred_element_type=jnp.float32)
    output = result.astype(jnp.bfloat16)[None]
    cotangent_low = cotangent[0]
    grad_out_full = cotangent_low.astype(jnp.float32)
    grad_down_full = jnp.einsum(
        "tf,td->fd", hidden_low, cotangent_low, preferred_element_type=jnp.float32
    )
    grad_hidden = jnp.einsum(
        "td,fd->tf", cotangent_low, down_full, preferred_element_type=jnp.float32
    )
    grad_gate_pre = (
        grad_hidden * up_pre * (sigmoid_gate * (1.0 + gate_pre * (1.0 - sigmoid_gate)))
    ).astype(jnp.bfloat16)
    grad_up_pre = (grad_hidden * silu_gate).astype(jnp.bfloat16)
    grad_gate_full = jnp.einsum(
        "td,tf->df", normed_two_low, grad_gate_pre, preferred_element_type=jnp.float32
    )
    grad_up_full = jnp.einsum(
        "td,tf->df", normed_two_low, grad_up_pre, preferred_element_type=jnp.float32
    )
    grad_normed_two = jnp.einsum(
        "tf,df->td", grad_gate_pre, gate_full, preferred_element_type=jnp.float32
    ) + jnp.einsum("tf,df->td", grad_up_pre, up_full, preferred_element_type=jnp.float32)
    grad_middle_norm, grad_gain_two = norm_backward(
        middle, inv_rms_two, norm_two_gain, grad_normed_two
    )
    grad_middle = grad_out_full + grad_middle_norm
    grad_branch = grad_middle.astype(jnp.bfloat16)
    grad_out_proj = jnp.einsum(
        "ta,td->ad", attention_low, grad_branch, preferred_element_type=jnp.float32
    )
    grad_attention = jnp.einsum(
        "td,ad->ta", grad_branch, out_full, preferred_element_type=jnp.float32
    )
    grad_attention = grad_attention.reshape(local_blocks, BLOCK, HEADS, VDIM)
    grad_numerator = (grad_attention / denominator[..., None]).astype(jnp.bfloat16)
    grad_denominator = (-jnp.sum(grad_attention * attention_full, axis=-1) / denominator).astype(
        jnp.bfloat16
    )
    grad_denom_wide = grad_denominator.astype(jnp.float32)
    grad_kernel = (
        jnp.einsum(
            "nshv,nthv->nhst", grad_numerator, value_blocks, preferred_element_type=jnp.float32
        )
        + jnp.transpose(grad_denom_wide, (0, 2, 1))[..., None]
    )
    grad_scores = ((1.0 + scores) * grad_kernel).astype(jnp.bfloat16)
    flat_numer = grad_numerator.reshape(row_count, HEADS * VDIM)
    flat_denom = grad_denominator.reshape(row_count, HEADS)
    running = (state_zero, norm_zero)
    query_piece = lax.all_gather(queries, "ctx", axis=0, tiled=True)
    numer_piece = lax.all_gather(flat_numer, "ctx", axis=0, tiled=True)
    denom_piece = lax.all_gather(flat_denom, "ctx", axis=0, tiled=True)
    block_count = query_piece.shape[0] // BLOCK
    group_size = block_group()
    others = positions
    query_groups = query_piece.reshape(block_count // group_size, group_size, BLOCK, HEADS, FDIM)
    numer_groups = numer_piece.reshape(block_count // group_size, group_size, BLOCK, HEADS, VDIM)
    denom_groups = denom_piece.reshape(block_count // group_size, group_size, BLOCK, HEADS)
    other_groups = others.reshape(block_count // group_size, group_size)

    def one_group(inner_sum, group_args):
        queries_here, numer_here, denom_here, places = group_args
        query_feat = features(queries_here.astype(jnp.float32) * 0.5).astype(jnp.bfloat16)
        grad_states = jnp.einsum(
            "gthf,gthv->ghfv", query_feat, numer_here, preferred_element_type=jnp.float32
        )
        grad_norms = jnp.einsum(
            "gthf,gth->ghf", query_feat, denom_here, preferred_element_type=jnp.float32
        )
        later_mask = (places[None, :] > own_positions[:, None]).astype(jnp.float32)
        return (
            (
                inner_sum[0]
                + jnp.einsum("ig,ghfv->ihfv", later_mask, grad_states, precision=highest),
                inner_sum[1] + jnp.einsum("ig,ghf->ihf", later_mask, grad_norms, precision=highest),
            ),
            None,
        )

    running, unused = lax.scan(
        one_group, running, (query_groups, numer_groups, denom_groups, other_groups)
    )
    later_states, later_norms = running
    grad_phi_query = (
        jnp.einsum("nshv,nhfv->nshf", grad_numerator.astype(jnp.float32), prefix, precision=highest)
        + grad_denom_wide[..., None] * prefix_norm[:, None, :, :]
    )
    grad_phi_key = (
        jnp.einsum(
            "nthv,nhfv->nthf", value_blocks.astype(jnp.float32), later_states, precision=highest
        )
        + later_norms[:, None, :, :]
    )
    grad_values = jnp.einsum(
        "nhst,nshv->nthv", kernel_low, grad_numerator, preferred_element_type=jnp.float32
    ) + jnp.einsum("nthf,nhfv->nthv", phi_key.astype(jnp.float32), later_states, precision=highest)
    grad_values_low = grad_values.reshape(row_count, HEADS * VDIM).astype(jnp.bfloat16)
    grad_queries = jnp.einsum(
        "nhst,nthf->nshf", grad_scores, key_blocks, preferred_element_type=jnp.float32
    ) * 0.25 + 0.5 * features_back(query_scaled, grad_phi_query)
    grad_queries_low = grad_queries.reshape(row_count, HEADS * FDIM).astype(jnp.bfloat16)
    grad_keys = jnp.einsum(
        "nhst,nshf->nthf", grad_scores, query_blocks, preferred_element_type=jnp.float32
    ) * 0.25 + 0.5 * features_back(key_scaled, grad_phi_key)
    grad_keys_low = grad_keys.reshape(row_count, HEADS * FDIM).astype(jnp.bfloat16)
    grad_query_full = jnp.einsum(
        "td,tk->dk", normed_one_low, grad_queries_low, preferred_element_type=jnp.float32
    )
    grad_key_full = jnp.einsum(
        "td,tk->dk", normed_one_low, grad_keys_low, preferred_element_type=jnp.float32
    )
    grad_value_full = jnp.einsum(
        "td,tk->dk", normed_one_low, grad_values_low, preferred_element_type=jnp.float32
    )
    grad_normed_one = (
        jnp.einsum("tk,dk->td", grad_queries_low, query_full, preferred_element_type=jnp.float32)
        + jnp.einsum("tk,dk->td", grad_keys_low, key_full, preferred_element_type=jnp.float32)
        + jnp.einsum("tk,dk->td", grad_values_low, value_full, preferred_element_type=jnp.float32)
    )
    grad_from_norm, grad_gain_one = norm_backward(
        residual, inv_rms_one, norm_one_gain, grad_normed_one
    )
    grad_tokens = (grad_middle + grad_from_norm)[None]
    shards = (
        lax.psum_scatter(
            grad_gain_one.astype(jnp.bfloat16), "fsdp", scatter_dimension=0, tiled=True
        ).astype(jnp.float32),
        lax.psum_scatter(
            grad_query_full.astype(jnp.bfloat16), "fsdp", scatter_dimension=0, tiled=True
        ).astype(jnp.float32),
        lax.psum_scatter(
            grad_key_full.astype(jnp.bfloat16), "fsdp", scatter_dimension=0, tiled=True
        ).astype(jnp.float32),
        lax.psum_scatter(
            grad_value_full.astype(jnp.bfloat16), "fsdp", scatter_dimension=0, tiled=True
        ).astype(jnp.float32),
        lax.psum_scatter(
            grad_out_proj.astype(jnp.bfloat16), "fsdp", scatter_dimension=0, tiled=True
        ).astype(jnp.float32),
        lax.psum_scatter(
            grad_gain_two.astype(jnp.bfloat16), "fsdp", scatter_dimension=0, tiled=True
        ).astype(jnp.float32),
        lax.psum_scatter(
            grad_gate_full.astype(jnp.bfloat16), "fsdp", scatter_dimension=0, tiled=True
        ).astype(jnp.float32),
        lax.psum_scatter(
            grad_up_full.astype(jnp.bfloat16), "fsdp", scatter_dimension=0, tiled=True
        ).astype(jnp.float32),
        lax.psum_scatter(
            grad_down_full.astype(jnp.bfloat16), "fsdp", scatter_dimension=0, tiled=True
        ).astype(jnp.float32),
    )
    totals = lax.psum(
        (
            shards[0],
            shards[1],
            shards[2],
            shards[3],
            shards[4],
            shards[5],
            shards[6],
            shards[7],
            shards[8],
        ),
        "ctx",
    )
    return (
        output,
        grad_tokens,
        totals[0],
        totals[1],
        totals[2],
        totals[3],
        totals[4],
        totals[5],
        totals[6],
        totals[7],
        totals[8],
    )


def solution(mesh):
    in_specs = (
        P("fsdp", "ctx", None),
        P("fsdp", None),
        P("fsdp"),
        P("fsdp", None),
        P("fsdp", None),
        P("fsdp", None),
        P("fsdp", None),
        P("fsdp"),
        P("fsdp", None),
        P("fsdp", None),
        P("fsdp", None),
        P("fsdp", "ctx", None),
    )
    out_specs = (
        P("fsdp", "ctx", None),
        P("fsdp", "ctx", None),
        P("fsdp"),
        P("fsdp", None),
        P("fsdp", None),
        P("fsdp", None),
        P("fsdp", None),
        P("fsdp"),
        P("fsdp", None),
        P("fsdp", None),
        P("fsdp", None),
    )
    return jax.shard_map(body, mesh=mesh, in_specs=in_specs, out_specs=out_specs, check_vma=False)
```

profile of v0, /device:TPU:0, one launch (start us, length us, event | category | flops | bytes accessed | tf_op | source)
XLA Modules:
  0.0 1292.5 jit_solution(17293718670228395038)
XLA Ops:
  8.6 6.0 all-gather
  16.1 9.3 all_gather.45
  28.8 7.1 all-gather.12.cloned.1.call-done
  42.4 7.3 all_gather.44
  81.6 7.7 all-gather.14.cloned.1.call-done
  96.9 118.5 %all-gather.16.cloned.1.call-done = bf16[4096,1024]{1,0:T(8,128)(2,1)} async-done(((bf16[512,1024]{1,0:T(8,128)(2,1)}), bf16[4096,1024]{1,0:T(8,128)(2,1)}) %all-gather.16.cloned.1.call-update) | async-done | bytes 8388624 | tf_op jit(solution)/shard_map/all_gather | solution.py:117
  215.5 22.2 %reshape.269 = bf16[2,8,256,16,64]{4,3,2,1,0:T(8,128)(2,1)} reshape(bf16[4096,1024]{1,0:T(8,128)(2,1)} %all-gather.16.cloned.1.call-done) | data formatting | bytes 16777216 | tf_op jit(solution)/shard_map/reshape | solution.py:122
  237.7 19.7 %copy.112 = bf16[2,8,256,16,64]{2,4,3,1,0:T(8,128)(2,1)} copy(bf16[2,8,256,16,64]{4,3,2,1,0:T(8,128)(2,1)} %reshape.269) | data formatting | bytes 16777216
  257.4 111.2 %while.26 = (s32[]{:T(128)}, f32[2,16,273,64]{2,0,3,1:T(2,128)S(1)}, f32[2,16,273]{2,0,1:T(2,128)S(1)}, s32[2,8]{1,0:T(2,128)S(1)}, s32[2]{0:T(128)S(1)}, /*inde...) while((s32[]{:T(128)}, ...), condition=%wide.region_3.4_spmd.clone, body=%wide.region_1.3_spmd.clone.sunk | while | flops 1343690752 | bytes 159030480 | solution.py:141
  264.4 5.8 copy-done
  270.2 8.2 convert_reduce_fusion.2
  278.4 13.8 %fusion.184 = f32[8,16,273,64]{2,3,1,0:T(8,128)} fusion(bf16[8,256,16,256]{1,3,2,0:T(8,128)(2,1)} %bitcast.288, bf16[8,256,16,16]{1,3,2,0:T(8,128)(2,1)} %copy-done.1, bf16[273]{0:T(512)(128)(2,1)S(1)} %pad.clone.2, bf16[2,8,256,16,64]{2,4,3,1,0:T(8,128)(2,1)} %get-tuple-element.396, s32[]{:T(128)S(6)} %copy.272), kind=kOutput, calls=%fused_computation.5.clone.1 | convolution fusion | flops 1198718976 | bytes 30966310 | tf_op jit(solution)/shard_map/while/body/eval_jaxpr/gthf,gthv->ghfv/dot_general | solution.py:128
  292.3 19.9 %select_add_fusion.4 = f32[2,16,273,64]{2,0,3,1:T(2,128)S(1)} fusion(f32[2,16,273,64]{2,0,3,1:T(2,128)S(1)} %get-tuple-element.380, pred[]{:T(512)S(6)} %compare.6, f32[8,16,273,64]{2,3,1,0:T(8,128)} %fusion.184, s32[8]{0:T(128)S(1)} %fusion.185, s32[2]{0:T(128)S(1)} %get-tuple-element.394), kind=kOutput, calls=%fused_computation.9.clone.1 | convolution fusion | flops 54792208 | bytes 13418537 | tf_op jit(solution)/shard_map/while/body/eval_jaxpr/ig,ghfv->ihfv/dot_general | solution.py:135
  319.4 5.8 copy-done
  325.2 8.2 convert_reduce_fusion.2
  333.4 15.2 %fusion.184 = f32[8,16,273,64]{2,3,1,0:T(8,128)} fusion(bf16[8,256,16,256]{1,3,2,0:T(8,128)(2,1)} %bitcast.288, bf16[8,256,16,16]{1,3,2,0:T(8,128)(2,1)} %copy-done.1, bf16[273]{0:T(512)(128)(2,1)S(1)} %pad.clone.2, bf16[2,8,256,16,64]{2,4,3,1,0:T(8,128)(2,1)} %get-tuple-element.396, s32[]{:T(128)S(6)} %copy.272), kind=kOutput, calls=%fused_computation.5.clone.1 | convolution fusion | flops 1198718976 | bytes 30966310 | tf_op jit(solution)/shard_map/while/body/eval_jaxpr/gthf,gthv->ghfv/dot_general | solution.py:128
  348.6 19.3 %select_add_fusion.4 = f32[2,16,273,64]{2,0,3,1:T(2,128)S(1)} fusion(f32[2,16,273,64]{2,0,3,1:T(2,128)S(1)} %get-tuple-element.380, pred[]{:T(512)S(6)} %compare.6, f32[8,16,273,64]{2,3,1,0:T(8,128)} %fusion.184, s32[8]{0:T(128)S(1)} %fusion.185, s32[2]{0:T(128)S(1)} %get-tuple-element.394), kind=kOutput, calls=%fused_computation.9.clone.1 | convolution fusion | flops 54792208 | bytes 13418537 | tf_op jit(solution)/shard_map/while/body/eval_jaxpr/ig,ghfv->ihfv/dot_general | solution.py:135
  389.7 8.5 fusion.122
  398.3 8.7 fusion.121
  407.0 12.3 multiply_convert_fusion.5
  427.1 6.2 fusion.123
  433.4 6.2 multiply_reduce_fusion
  457.8 6.4 bitcast_add_fusion
  470.3 16.5 %fusion.44 = f32[2,256,16,16]{1,3,2,0:T(8,128)S(1)} fusion(f32[2,256,16,16,16]{1,4,3,2,0:T(8,128)} %bitcast.293, f32[2,256,16,16]{1,3,2,0:T(8,128)S(1)} %copy-done.21), kind=kLoop, calls=%fused_computation.67 | loop fusion | flops 6160384 | bytes 9437184 | tf_op jit(solution)/shard_map/...ab,...b->...a/dot_general | solution.py:30
  486.8 5.7 multiply_convert_fusion.3
  502.1 7.6 convolution_convert_fusion.2
  511.5 6.2 convolution_convert_fusion
  530.6 31.4 %all_gather.55 = bf16[4096,16]{0,1:T(8,128)(2,1)S(1)} all-gather(bf16[512,16]{0,1:T(8,128)(2,1)S(1)} %bitcast.321), channel_id=1, replica_groups=mesh['ctx'=8,'fsdp'=4] {'ctx'}, dimensions={0}, use_global_device_ids=true | all-gather | bytes 147456 | tf_op jit(solution)/shard_map/all_gather | solution.py:218
  569.9 22.2 %reshape.271 = bf16[2,8,256,16,64]{4,3,2,1,0:T(8,128)(2,1)} reshape(bf16[4096,1024]{1,0:T(8,128)(2,1)} %all-gather.28.cloned.1.call-done) | data formatting | bytes 16777216 | tf_op jit(solution)/shard_map/reshape | solution.py:223
  592.1 19.7 %copy.135 = bf16[2,8,256,16,64]{2,4,3,1,0:T(8,128)(2,1)} copy(bf16[2,8,256,16,64]{4,3,2,1,0:T(8,128)(2,1)} %reshape.271) | data formatting | bytes 16777216
  611.7 114.5 %while.27 = (s32[]{:T(128)}, f32[2,16,273,64]{2,0,3,1:T(2,128)S(1)}, f32[2,16,273]{2,0,1:T(2,128)S(1)}, s32[2,8]{1,0:T(2,128)S(1)}, s32[2]{0:T(128)S(1)}, /*inde...) while((s32[]{:T(128)}, ...), condition=%wide.region_9.10_spmd.clone, body=%wide.region_8.9_spmd.clone.sunk | while | flops 1352671360 | bytes 92249264 | solution.py:246
  614.5 8.8 multiply_convert_fusion.12
  623.3 9.2 fusion.193
  632.5 16.2 %fusion.191 = f32[8,16,273,64]{2,3,1,0:T(8,128)} fusion(bf16[8,256,16,256]{1,3,2,0:T(8,128)(2,1)} %bitcast.290, bf16[8,256,16,16]{1,3,2,0:T(8,128)(2,1)} %copy-done.9, bf16[273]{0:T(512)(128)(2,1)S(1)} %pad.3.clone.2, bf16[2,8,256,16,64]{2,4,3,1,0:T(8,128)(2,1)} %get-tuple-element.431, s32[]{:T(128)S(6)} %copy.281), kind=kOutput, calls=%fused_computation.30.clone.1 | convolution fusion | flops 1198718976 | bytes 30966310 | tf_op jit(solution)/shard_map/while/body/eval_jaxpr/gthf,gthv->ghfv/dot_general | solution.py:230
  648.8 19.8 %select_add_fusion.5 = f32[2,16,273,64]{2,0,3,1:T(2,128)S(1)} fusion(f32[2,16,273,64]{2,0,3,1:T(2,128)S(1)} %get-tuple-element.414, pred[]{:T(512)S(6)} %compare.7, f32[8,16,273,64]{2,3,1,0:T(8,128)} %fusion.191, s32[8]{0:T(128)S(1)} %fusion.192, s32[2]{0:T(128)S(1)} %get-tuple-element.429), kind=kOutput, calls=%fused_computation.35.clone.1 | convolution fusion | flops 54792208 | bytes 13418537 | tf_op jit(solution)/shard_map/while/body/eval_jaxpr/ig,ghfv->ihfv/dot_general | solution.py:240
  671.6 8.8 multiply_convert_fusion.12
  680.4 9.3 fusion.193
  689.7 16.1 %fusion.191 = f32[8,16,273,64]{2,3,1,0:T(8,128)} fusion(bf16[8,256,16,256]{1,3,2,0:T(8,128)(2,1)} %bitcast.290, bf16[8,256,16,16]{1,3,2,0:T(8,128)(2,1)} %copy-done.9, bf16[273]{0:T(512)(128)(2,1)S(1)} %pad.3.clone.2, bf16[2,8,256,16,64]{2,4,3,1,0:T(8,128)(2,1)} %get-tuple-element.431, s32[]{:T(128)S(6)} %copy.281), kind=kOutput, calls=%fused_computation.30.clone.1 | convolution fusion | flops 1198718976 | bytes 30966310 | tf_op jit(solution)/shard_map/while/body/eval_jaxpr/gthf,gthv->ghfv/dot_general | solution.py:230
  705.7 19.7 %select_add_fusion.5 = f32[2,16,273,64]{2,0,3,1:T(2,128)S(1)} fusion(f32[2,16,273,64]{2,0,3,1:T(2,128)S(1)} %get-tuple-element.414, pred[]{:T(512)S(6)} %compare.7, f32[8,16,273,64]{2,3,1,0:T(8,128)} %fusion.191, s32[8]{0:T(128)S(1)} %fusion.192, s32[2]{0:T(128)S(1)} %get-tuple-element.429), kind=kOutput, calls=%fused_computation.35.clone.1 | convolution fusion | flops 54792208 | bytes 13418537 | tf_op jit(solution)/shard_map/while/body/eval_jaxpr/ig,ghfv->ihfv/dot_general | solution.py:240
  726.2 6.9 add_bitcast_fusion
  739.2 17.3 %fusion.41 = f32[2,256,16,16]{1,3,2,0:T(8,128)} fusion(f32[2,256,16,16,16]{1,4,3,2,0:T(8,128)} %bitcast.294, f32[2,256,16,16]{1,3,2,0:T(8,128)S(1)} %copy-done.23), kind=kLoop, calls=%fused_computation.63 | loop fusion | flops 6160384 | bytes 9437184 | tf_op jit(solution)/shard_map/...ab,...b->...a/dot_general | solution.py:30
  761.8 8.4 fusion.48
  770.3 6.2 fusion.81
  785.7 7.7 fusion.80
  803.5 5.9 all-reduce.3
  813.0 7.9 reduce-scatter.10.cloned.1.call-done
  820.9 34.4 %reduce-scatter.12.cloned.1.call-done = bf16[256,1024]{1,0:T(8,128)(2,1)} async-done(((bf16[1024,1024]{1,0:T(8,128)(2,1)}), bf16[256,1024]{1,0:T(8,128)(2,1)}) %reduce-scatter.12.cloned.1.call-update) | async-done | bytes 524304 | tf_op jit(solution)/shard_map/reduce_scatter | solution.py:300
  855.3 430.5 %all-reduce.5 = (f32[256]{0:T(256)}, f32[256,256]{1,0:T(8,128)}, f32[256,256]{1,0:T(8,128)}, f32[256,1024]{1,0:T(8,128)}, f32[256,1024]{1,0:T(8,128)}, /*index=5...) all-reduce(f32[256]{0:T(256)S(1)} %get-tuple-element.267, ...), channel_id=1, replica_groups=mesh['ctx'=8,'fsdp'=4] {'ctx'}, use_global_device_ids=true, to_apply=%region_13.14 | all-reduce | flops 2769408 | bytes 16617472 | tf_op jit(solution)/shard_map/psum | solution.py:319
  (302 shorter events, 190.8 us)
Async XLA Ops:
  7.2 28.8 %copy-start.11 = (bf16[1,512,1024]{2,1,0:T(8,128)(2,1)S(1)}, bf16[1,512,1024]{2,1,0:T(8,128)(2,1)}, u32[]{:S(2)}) copy-start(bf16[1,512,1024]{2,1,0:T(8,128)(2,1)} %param.16) | copy-start | bytes 3145732
  7.2 28.7 %all-gather.12.cloned.1.call-start = ((), (), s32[]{:S(2)}) async-start(), calls=%async_computation.7 | async-start | bytes 2621440 | tf_op jit(solution)/shard_map/all_gather | solution.py:71
  7.9 81.4 %all-gather.14.cloned.1.call-start = ((), (), s32[]{:S(2)}) async-start(), calls=%async_computation.8 | async-start | bytes 2359296 | tf_op jit(solution)/shard_map/all_gather | solution.py:116
  14.6 35.1 %copy-start.53 = (f32[4,1,256]{2,1,0:T(1,128)}, f32[4,1,256]{2,1,0:T(1,128)S(1)}, u32[]{:S(2)}) copy-start(f32[4,1,256]{2,1,0:T(1,128)S(1)} %convert_element_type.281) | copy-start | bytes 12292
  26.1 23.6 %copy-start.58 = (f32[512]{0:T(512)}, f32[512]{0:T(512)S(1)}, u32[]{:S(2)}) copy-start(f32[512]{0:T(512)S(1)} %get-tuple-element.253) | copy-start | bytes 6148
  28.7 186.7 %all-gather.16.cloned.1.call-start = ((), (), s32[]{:S(2)}) async-start(), calls=%async_computation.9 | async-start | bytes 9437184 | tf_op jit(solution)/shard_map/all_gather | solution.py:117
  39.8 343.9 %all-gather.18.cloned.1.call-start = ((), (), s32[]{:S(2)}) async-start(), calls=%async_computation.10 | async-start | bytes 2621440 | tf_op jit(solution)/shard_map/all_gather | solution.py:72
  40.4 13.2 %copy-start.39 = (bf16[512,256]{1,0:T(8,128)(2,1)S(1)}, bf16[512,256]{1,0:T(8,128)(2,1)}, u32[]{:S(2)}) copy-start(bf16[512,256]{1,0:T(8,128)(2,1)} %convolution_convert_fusion.8) | copy-start | bytes 786436
  40.4 349.3 %all-gather.22.cloned.1.call-start = ((), (), s32[]{:S(2)}) async-start(), calls=%async_computation.12 | async-start | bytes 7045120 | tf_op jit(solution)/shard_map/all_gather | solution.py:75
  41.0 13.4 %copy-start.66 = (s32[1,16]{1,0:T(1,128)S(1)}, s32[1,16]{1,0:T(1,128)}, u32[]{:S(2)}) copy-start(s32[1,16]{1,0:T(1,128)} %param.17) | copy-start | bytes 196
  41.0 14.7 %copy-start.67 = (bf16[256]{0:T(256)(128)(2,1)S(1)}, bf16[256]{0:T(256)(128)(2,1)}, u32[]{:S(2)}) copy-start(bf16[256]{0:T(256)(128)(2,1)} %param.23) | copy-start | bytes 1540
  41.0 357.3 %all-gather.20.cloned.1.call-start = ((), (), s32[]{:S(2)}) async-start(), calls=%async_computation.11 | async-start | bytes 7045120 | tf_op jit(solution)/shard_map/all_gather | solution.py:74
  41.6 365.4 %all-gather.24.cloned.1.call-start = ((), (), s32[]{:S(2)}) async-start(), calls=%async_computation.13 | async-start | bytes 7045120 | tf_op jit(solution)/shard_map/all_gather | solution.py:76
  42.3 480.5 %all-gather.26.cloned.1.call-start = ((), (), s32[]{:S(2)}) async-start(), calls=%async_computation.14 | async-start | bytes 2359296 | tf_op jit(solution)/shard_map/all_gather | solution.py:216
  51.7 518.2 %all-gather.28.cloned.1.call-start = ((), (), s32[]{:S(2)}) async-start(), calls=%async_computation.15 | async-start | bytes 9437184 | tf_op jit(solution)/shard_map/all_gather | solution.py:217
  62.4 11.1 copy-start.28
  65.0 8.5 copy-start.20
  257.3 111.2 %copy-start.64 = (bf16[273]{0:T(512)(128)(2,1)S(1)}, bf16[273]{0:T(512)(128)(2,1)}, u32[]{:S(2)}) copy-start(bf16[273]{0:T(512)(128)(2,1)} %pad.9.clone) | copy-start | bytes 1642
  368.6 9.7 slice-start
  387.8 10.4 copy-start.56
  427.1 6.2 copy-start.24
  427.1 6.2 copy-start.51
  427.1 6.3 copy-start.57
  433.3 6.3 copy-start.36
  433.3 6.3 copy-start.62
  444.8 348.6 %reduce-scatter.8.cloned.1.call-start = ((), (), s32[]{:S(2)}) async-start(), calls=%async_computation.16 | async-start | bytes 655360 | tf_op jit(solution)/shard_map/reduce_scatter | solution.py:294
  457.1 29.7 %copy-start.10 = (bf16[2,256,16,64]{1,3,2,0:T(8,128)(2,1)}, bf16[2,256,16,64]{1,3,2,0:T(8,128)(2,1)S(1)}, u32[]{:S(2)}) copy-start(bf16[2,256,16,64]{1,3,2,0:T(8,128)(2,1)S(1)} %get-tuple-element.246) | copy-start | bytes 3145732
  470.3 16.5 %copy-start.16 = (bf16[2,256,16,64]{1,3,2,0:T(8,128)(2,1)S(1)}, bf16[2,256,16,64]{1,3,2,0:T(8,128)(2,1)}, u32[]{:S(2)}) copy-start(bf16[2,256,16,64]{1,3,2,0:T(8,128)(2,1)} %copy.107) | copy-start | bytes 3145732
  486.8 7.8 copy-start.31
  499.4 294.0 %reduce-scatter.14.cloned.1.call-start = ((), (), s32[]{:S(2)}) async-start(), calls=%async_computation.19 | async-start | bytes 2621440 | tf_op jit(solution)/shard_map/reduce_scatter | solution.py:303
  502.1 291.3 %reduce-scatter.20.cloned.1.call-start = ((), (), s32[]{:S(2)}) async-start(), calls=%async_computation.22 | async-start | bytes 7045120 | tf_op jit(solution)/shard_map/reduce_scatter | solution.py:315
  509.7 283.7 %reduce-scatter.18.cloned.1.call-start = ((), (), s32[]{:S(2)}) async-start(), calls=%async_computation.21 | async-start | bytes 7045120 | tf_op jit(solution)/shard_map/reduce_scatter | solution.py:312
  517.7 278.4 %reduce-scatter.16.cloned.1.call-start = ((), (), s32[]{:S(2)}) async-start(), calls=%async_computation.20 | async-start | bytes 7045120 | tf_op jit(solution)/shard_map/reduce_scatter | solution.py:309
  522.8 7.8 copy-start.52
  526.9 35.8 %copy-start.37 = (bf16[512,1024]{1,0:T(8,128)(2,1)S(1)}, bf16[512,1024]{1,0:T(8,128)(2,1)}, u32[]{:S(2)}) copy-start(bf16[512,1024]{1,0:T(8,128)(2,1)} %multiply_convert_fusion.8) | copy-start | bytes 3145732
  526.9 35.8 %copy-start.71 = (bf16[512,2752]{0,1:T(8,128)(2,1)S(1)}, bf16[512,2752]{0,1:T(8,128)(2,1)}, u32[]{:S(2)}) copy-start(bf16[512,2752]{0,1:T(8,128)(2,1)} %get-tuple-element.244) | copy-start | bytes 8454148
  567.6 253.3 %reduce-scatter.10.cloned.1.call-start = ((), (), s32[]{:S(2)}) async-start(), calls=%async_computation.17 | async-start | bytes 655360 | tf_op jit(solution)/shard_map/reduce_scatter | solution.py:297
  592.0 19.7 %copy-start.46 = (s32[2]{0:T(128)S(1)}, s32[2]{0:T(128)}, u32[]{:S(2)}) copy-start(s32[2]{0:T(128)} %copy-done.45) | copy-start | bytes 28
  592.0 19.7 %copy-start.69 = (s32[2,8]{1,0:T(2,128)S(1)}, s32[2,8]{1,0:T(2,128)}, u32[]{:S(2)}) copy-start(s32[2,8]{1,0:T(2,128)} %copy-done.68) | copy-start | bytes 196
  614.5 8.8 copy-start.9
  671.6 8.8 copy-start.9
  739.2 17.3 %copy-start.3 = (bf16[2,16,256,256]{2,3,1,0:T(8,128)(2,1)S(1)}, bf16[2,16,256,256]{2,3,1,0:T(8,128)(2,1)}, u32[]{:S(2)}) copy-start(bf16[2,16,256,256]{2,3,1,0:T(8,128)(2,1)} %copy-done.2) | copy-start | bytes 12582916
  739.2 17.3 %copy-start.29 = (bf16[2,256,16,16]{1,0,3,2:T(2,128)(2,1)S(1)}, bf16[2,256,16,16]{1,0,3,2:T(2,128)(2,1)}, u32[]{:S(2)}) copy-start(bf16[2,256,16,16]{1,0,3,2:T(2,128)(2,1)} %copy-done.28) | copy-start | bytes 786436
  770.2 85.1 %reduce-scatter.12.cloned.1.call-start = ((), (), s32[]{:S(2)}) async-start(), calls=%async_computation.18 | async-start | bytes 2621440 | tf_op jit(solution)/shard_map/reduce_scatter | solution.py:300
  778.8 6.9 copy-start.8
  799.3 10.2 copy-start.19
  799.4 10.2 copy-start.61
  803.5 51.8 %copy-start.48 = (bf16[256,256]{1,0:T(8,128)(2,1)S(1)}, bf16[256,256]{1,0:T(8,128)(2,1)}, u32[]{:S(2)}) copy-start(bf16[256,256]{1,0:T(8,128)(2,1)} %reduce-scatter.8.cloned.1.call-done) | copy-start | bytes 393220
  (45 other events, 174.0 us)
Sparse Core Ops, SparseCore 0:
  9.6 26.2 all-gather.11
  38.6 50.6 all-gather.13
  92.0 123.4 all-gather.15
  216.9 20.7 all-gather.17
  239.1 43.3 all-gather.21
  283.9 43.3 all-gather.19
  328.9 42.6 all-gather.23
  373.7 49.2 all-gather.25
  444.9 124.8 all-gather.27
  572.2 20.0 reduce-scatter.7
  594.9 31.4 reduce-scatter.13
  628.8 54.0 reduce-scatter.19
  685.6 53.9 reduce-scatter.17
  742.1 54.0 reduce-scatter.15
  799.2 21.6 reduce-scatter.9
  823.8 31.4 reduce-scatter.11
where the time goes:
time: 1300 us; the launch traced here: 1290 us
  blocking collectives  495 us (38%)
  matrix products  317 us (24%)
  waiting for transfers between devices  184 us (14%)
  local copies, waits for them, and re-layouts  168 us (13%)
  other arithmetic  111 us (9%)
  between operations  15.6 us (1%)
    psum x1, blocking collectives, body(): lax.psum((shards[0], shards[1], shards[2], shards[3], shards[4], shards[5...  430 us
    all_gather x1, waiting for transfers between devices, body(): value_piece = lax.all_gather(values_all, 'ctx', axis=0, tiled=True)  119 us
    unnamed x156, local copies, waits for them, and re-layouts  63.5 us
    dot_general x2, matrix products, one_group(): jnp.einsum('ig,ghfv->ihfv', later_mask, grad_states, precision=highest)  39.6 us
    dot_general x2, matrix products, one_group(): jnp.einsum('ig,ghfv->ihfv', earlier, states, precision=highest)  39.2 us
    another operation x12, other arithmetic  37.8 us
    reduce_scatter x1, waiting for transfers between devices, body(): lax.psum_scatter(grad_value_full.astype(jnp.bfloat16), 'fsdp', scatter_di...  34.4 us
    dot_general x2, other arithmetic, features_back(): jnp.einsum('...ab,...b->...a', square + jnp.swapaxes(square, -1, -2), sca...  33.7 us
  transfers between devices with their start and end apart: 16, of which 7 were waited for; matrix products, arithmetic and copies ran while one was open for 44% of the time, Pallas kernels for 0%

commit v1 on v0

--- a/solution.py
+++ b/solution.py
@@ -114,7 +114,9 @@
     norm_zero = jnp.zeros((local_blocks, HEADS, feat_width), jnp.float32)
     running = (state_zero, norm_zero)
     key_piece = lax.all_gather(keys_all, "ctx", axis=0, tiled=True)
-    value_piece = lax.all_gather(values_all, "ctx", axis=0, tiled=True)
+    value_piece = jnp.concatenate(
+        lax.all_to_all(jnp.stack([values_all] * lax.axis_size("ctx")), "ctx", 0, 0), axis=0
+    )
     block_count = key_piece.shape[0] // BLOCK
     group_size = block_group()
     others = positions

time: 1300 us -> 1330 us (1.023)
  waiting for transfers between devices: 184 us -> 227 us
  local copies, waits for them, and re-layouts: 168 us -> 140 us
  other arithmetic: 111 us -> 129 us
    all_gather x1 -> x0, waiting for transfers between devices: 119 us -> none  [body(): value_piece = lax.all_gather(values_all, 'ctx', axis=0, tiled=True)]
    all_to_all x0 -> x1, waiting for transfers between devices: none -> 83.4 us  [body(): lax.all_to_all(jnp.stack([values_all] * lax.axis_size('ctx')), 'ctx', 0, 0)]
    all_gather x1, waiting for transfers between devices: 7.69 us -> 82.5 us  [body(): key_piece = lax.all_gather(keys_all, 'ctx', axis=0, tiled=True)]
    reshape x1 -> x0, local copies, waits for them, and re-layouts: 22.2 us -> none  [body(): value_piece.reshape(block_count // group_size, group_size, BLOCK, HEADS,...]
    unnamed x156 -> x157, local copies, waits for them, and re-layouts: 63.5 us -> 44.1 us
    another operation x0 -> x2, local copies, waits for them, and re-layouts: none -> 17 us  [the longest x1 13 us: body(): value_piece.reshape(block_count // group_size, group_size, BLOCK, HEADS,...]
  transfers between devices with their start and end apart: 16 -> 16, of which waited for: 7 -> 7; matrix products, arithmetic and copies ran while one was open for 44% -> 43% of each run, Pallas kernels for 0% -> 0%
where the time goes in v1:
time: 1330 us
  blocking collectives  496 us (37%)
  matrix products  312 us (23%)
  waiting for transfers between devices  227 us (17%)
  local copies, waits for them, and re-layouts  140 us (11%)
  other arithmetic  129 us (10%)
  between operations  15.6 us (1%)
    psum x1, blocking collectives, body(): lax.psum((shards[0], shards[1], shards[2], shards[3], shards[4], shards[5...  430 us
    all_to_all x1, waiting for transfers between devices, body(): lax.all_to_all(jnp.stack([values_all] * lax.axis_size('ctx')), 'ctx', 0, 0)  83.4 us
    all_gather x1, waiting for transfers between devices, body(): key_piece = lax.all_gather(keys_all, 'ctx', axis=0, tiled=True)  82.5 us
    another operation x12, other arithmetic  49 us
    unnamed x157, local copies, waits for them, and re-layouts  44.1 us
    dot_general x2, matrix products, one_group(): jnp.einsum('ig,ghfv->ihfv', later_mask, grad_states, precision=highest)  41.2 us
    dot_general x2, matrix products, one_group(): jnp.einsum('ig,ghfv->ihfv', earlier, states, precision=highest)  38.8 us
    reduce_scatter x1, waiting for transfers between devices, body(): lax.psum_scatter(grad_value_full.astype(jnp.bfloat16), 'fsdp', scatter_di...  34.4 us
  transfers between devices with their start and end apart: 16, of which 7 were waited for; matrix products, arithmetic and copies ran while one was open for 43% of the time, Pallas kernels for 0%

profile of v1, /device:TPU:0, one launch (start us, length us, event | category | flops | bytes accessed | tf_op | source)
XLA Modules:
  0.0 1328.2 jit_solution(4195033928369212909)
XLA Ops:
  8.7 6.0 all-gather
  16.2 9.4 all_gather.42
  43.5 6.0 all-to-all-start
  50.2 7.2 all_gather.41
  83.5 82.5 %all-gather.13.cloned.1.call-done = bf16[4096,256]{1,0:T(8,128)(2,1)} async-done(((bf16[512,256]{1,0:T(8,128)(2,1)}), bf16[4096,256]{1,0:T(8,128)(2,1)}) %all-gather.13.cloned.1.call-update) | async-done | bytes 2097168 | tf_op jit(solution)/shard_map/all_gather | solution.py:116
  173.6 83.4 %all-to-all-done = bf16[8,512,1024]{1,2,0:T(8,128)(2,1)} async-done(((bf16[8,512,1024]{1,2,0:T(8,128)(2,1)}), bf16[8,512,1024]{1,2,0:T(8,128)(2,1)}, u32[]{:S(2)}, u32[]{:S(2)}) %all-to-all-start) | async-done | bytes 8388640 | tf_op jit(solution)/shard_map/all_to_all | solution.py:118
  257.0 11.6 copy.111
  268.6 13.0 reshape_reshape.3
  281.6 122.0 %while.26 = (s32[]{:T(128)}, f32[2,16,273,64]{2,0,3,1:T(2,128)S(1)}, f32[2,16,273]{2,0,1:T(2,128)S(1)}, s32[2,8]{1,0:T(2,128)S(1)}, s32[2]{0:T(128)S(1)}, /*inde...) while((s32[]{:T(128)}, ...), condition=%wide.region_3.4_spmd.clone, body=%wide.region_1.3_spmd.clone.sunk | while | flops 1343690752 | bytes 125476048 | solution.py:143
  284.4 8.8 multiply_convert_fusion.11
  295.7 15.8 %fusion.179 = f32[8,16,273,64]{2,3,1,0:T(8,128)} fusion(bf16[8,256,16,256]{1,3,2,0:T(8,128)(2,1)} %bitcast.288, bf16[8,256,16,16]{1,3,2,0:T(8,128)(2,1)} %get-tuple-element.357, bf16[273]{0:T(512)(128)(2,1)S(1)} %pad.clone.2, bf16[1,8,256,16,64]{2,1,0,4,3:T(8,128)(2,1)} %constant_dynamic-slice_fusion.11), kind=kOutput, calls=%fused_computation.5.clone.1 | convolution fusion | flops 1198718976 | bytes 30966306 | tf_op jit(solution)/shard_map/while/body/eval_jaxpr/gthf,gthv->ghfv/dot_general | solution.py:130
  311.5 19.4 %select_add_fusion.4 = f32[2,16,273,64]{2,0,3,1:T(2,128)S(1)} fusion(f32[2,16,273,64]{2,0,3,1:T(2,128)S(1)} %get-tuple-element.380, pred[]{:T(512)S(6)} %compare.6, f32[8,16,273,64]{2,3,1,0:T(8,128)} %fusion.179, s32[8]{0:T(128)S(1)} %fusion.180, s32[2]{0:T(128)S(1)} %get-tuple-element.394), kind=kOutput, calls=%fused_computation.8.clone.1 | convolution fusion | flops 54792208 | bytes 13418537 | tf_op jit(solution)/shard_map/while/body/eval_jaxpr/ig,ghfv->ihfv/dot_general | solution.py:137
  330.9 11.8 convert_reduce_fusion.2
  345.8 8.8 multiply_convert_fusion.11
  357.0 14.6 %fusion.179 = f32[8,16,273,64]{2,3,1,0:T(8,128)} fusion(bf16[8,256,16,256]{1,3,2,0:T(8,128)(2,1)} %bitcast.288, bf16[8,256,16,16]{1,3,2,0:T(8,128)(2,1)} %get-tuple-element.357, bf16[273]{0:T(512)(128)(2,1)S(1)} %pad.clone.2, bf16[1,8,256,16,64]{2,1,0,4,3:T(8,128)(2,1)} %constant_dynamic-slice_fusion.11), kind=kOutput, calls=%fused_computation.5.clone.1 | convolution fusion | flops 1198718976 | bytes 30966306 | tf_op jit(solution)/shard_map/while/body/eval_jaxpr/gthf,gthv->ghfv/dot_general | solution.py:130
  371.6 19.4 %select_add_fusion.4 = f32[2,16,273,64]{2,0,3,1:T(2,128)S(1)} fusion(f32[2,16,273,64]{2,0,3,1:T(2,128)S(1)} %get-tuple-element.380, pred[]{:T(512)S(6)} %compare.6, f32[8,16,273,64]{2,3,1,0:T(8,128)} %fusion.179, s32[8]{0:T(128)S(1)} %fusion.180, s32[2]{0:T(128)S(1)} %get-tuple-element.394), kind=kOutput, calls=%fused_computation.8.clone.1 | convolution fusion | flops 54792208 | bytes 13418537 | tf_op jit(solution)/shard_map/while/body/eval_jaxpr/ig,ghfv->ihfv/dot_general | solution.py:137
  391.0 11.8 convert_reduce_fusion.2
  424.7 8.5 fusion.121
  433.2 8.5 fusion.122
  441.7 12.3 multiply_convert_fusion.5
  461.7 6.2 fusion.123
  468.0 6.2 multiply_reduce_fusion
  492.3 6.4 bitcast_add_fusion
  504.9 16.4 %fusion.41 = f32[2,256,16,16]{1,3,2,0:T(8,128)S(1)} fusion(f32[2,256,16,16,16]{1,4,3,2,0:T(8,128)} %bitcast.296, f32[2,256,16,16]{1,3,2,0:T(8,128)S(1)} %copy-done.21), kind=kLoop, calls=%fused_computation.66 | loop fusion | flops 6160384 | bytes 9437184 | tf_op jit(solution)/shard_map/...ab,...b->...a/dot_general | solution.py:30
  536.6 7.6 convolution_convert_fusion.1
  546.0 6.2 convolution_convert_fusion
  565.0 31.4 %all_gather.51 = bf16[4096,16]{0,1:T(8,128)(2,1)S(1)} all-gather(bf16[512,16]{0,1:T(8,128)(2,1)S(1)} %bitcast.325), channel_id=1, replica_groups=mesh['ctx'=8,'fsdp'=4] {'ctx'}, dimensions={0}, use_global_device_ids=true | all-gather | bytes 147456 | tf_op jit(solution)/shard_map/all_gather | solution.py:220
  605.5 22.2 %reshape.268 = bf16[2,8,256,16,64]{4,3,2,1,0:T(8,128)(2,1)} reshape(bf16[4096,1024]{1,0:T(8,128)(2,1)} %all-gather.25.cloned.1.call-done) | data formatting | bytes 16777216 | tf_op jit(solution)/shard_map/reshape | solution.py:225
  627.7 19.7 %copy.136 = bf16[2,8,256,16,64]{2,4,3,1,0:T(8,128)(2,1)} copy(bf16[2,8,256,16,64]{4,3,2,1,0:T(8,128)(2,1)} %reshape.268) | data formatting | bytes 16777216
  647.4 111.1 %while.27 = (s32[]{:T(128)}, f32[2,16,273,64]{2,0,3,1:T(2,128)S(1)}, f32[2,16,273]{2,0,1:T(2,128)S(1)}, s32[2,8]{1,0:T(2,128)S(1)}, s32[2]{0:T(128)S(1)}, /*inde...) while((s32[]{:T(128)}, ...), condition=%wide.region_9.10_spmd.clone, body=%wide.region_8.9_spmd.clone.sunk | while | flops 1352671360 | bytes 92249264 | solution.py:248
  650.2 8.7 multiply_convert_fusion.12
  659.0 13.5 %fusion.186 = f32[8,16,273,64]{2,3,1,0:T(8,128)} fusion(bf16[8,256,16,256]{1,3,2,0:T(8,128)(2,1)} %bitcast.290, bf16[8,256,16,16]{1,3,2,0:T(8,128)(2,1)} %get-tuple-element.367, bf16[273]{0:T(512)(128)(2,1)S(1)} %pad.3.clone.2, bf16[2,8,256,16,64]{2,4,3,1,0:T(8,128)(2,1)} %get-tuple-element.431, s32[]{:T(128)S(6)} %copy.291), kind=kOutput, calls=%fused_computation.29.clone.1 | convolution fusion | flops 1198718976 | bytes 30966310 | tf_op jit(solution)/shard_map/while/body/eval_jaxpr/gthf,gthv->ghfv/dot_general | solution.py:232
  672.4 20.5 %select_add_fusion.5 = f32[2,16,273,64]{2,0,3,1:T(2,128)S(1)} fusion(f32[2,16,273,64]{2,0,3,1:T(2,128)S(1)} %get-tuple-element.414, pred[]{:T(512)S(6)} %compare.7, f32[8,16,273,64]{2,3,1,0:T(8,128)} %fusion.186, s32[8]{0:T(128)S(1)} %fusion.187, s32[2]{0:T(128)S(1)} %get-tuple-element.429), kind=kOutput, calls=%fused_computation.34.clone.1 | convolution fusion | flops 54792208 | bytes 13418537 | tf_op jit(solution)/shard_map/while/body/eval_jaxpr/ig,ghfv->ihfv/dot_general | solution.py:242
  693.0 9.3 fusion.188
  705.4 8.7 multiply_convert_fusion.12
  714.1 13.7 %fusion.186 = f32[8,16,273,64]{2,3,1,0:T(8,128)} fusion(bf16[8,256,16,256]{1,3,2,0:T(8,128)(2,1)} %bitcast.290, bf16[8,256,16,16]{1,3,2,0:T(8,128)(2,1)} %get-tuple-element.367, bf16[273]{0:T(512)(128)(2,1)S(1)} %pad.3.clone.2, bf16[2,8,256,16,64]{2,4,3,1,0:T(8,128)(2,1)} %get-tuple-element.431, s32[]{:T(128)S(6)} %copy.291), kind=kOutput, calls=%fused_computation.29.clone.1 | convolution fusion | flops 1198718976 | bytes 30966310 | tf_op jit(solution)/shard_map/while/body/eval_jaxpr/gthf,gthv->ghfv/dot_general | solution.py:232
  727.8 20.7 %select_add_fusion.5 = f32[2,16,273,64]{2,0,3,1:T(2,128)S(1)} fusion(f32[2,16,273,64]{2,0,3,1:T(2,128)S(1)} %get-tuple-element.414, pred[]{:T(512)S(6)} %compare.7, f32[8,16,273,64]{2,3,1,0:T(8,128)} %fusion.186, s32[8]{0:T(128)S(1)} %fusion.187, s32[2]{0:T(128)S(1)} %get-tuple-element.429), kind=kOutput, calls=%fused_computation.34.clone.1 | convolution fusion | flops 54792208 | bytes 13418537 | tf_op jit(solution)/shard_map/while/body/eval_jaxpr/ig,ghfv->ihfv/dot_general | solution.py:242
  748.5 9.2 fusion.188
  758.5 6.9 add_bitcast_fusion
  771.5 17.3 %fusion.38 = f32[2,256,16,16]{1,3,2,0:T(8,128)} fusion(f32[2,256,16,16,16]{1,4,3,2,0:T(8,128)} %bitcast.297, f32[2,256,16,16]{1,3,2,0:T(8,128)S(1)} %copy-done.23), kind=kLoop, calls=%fused_computation.62 | loop fusion | flops 6160384 | bytes 9437184 | tf_op jit(solution)/shard_map/...ab,...b->...a/dot_general | solution.py:30
  794.2 7.7 fusion.45
  802.0 6.1 fusion.78
  817.4 7.6 fusion.77
  825.0 6.8 reduce-scatter.20.cloned.1.call-done
  839.3 5.9 all-reduce.3
  848.7 7.9 reduce-scatter.10.cloned.1.call-done
  856.6 34.4 %reduce-scatter.12.cloned.1.call-done = bf16[256,1024]{1,0:T(8,128)(2,1)} async-done(((bf16[1024,1024]{1,0:T(8,128)(2,1)}), bf16[256,1024]{1,0:T(8,128)(2,1)}) %reduce-scatter.12.cloned.1.call-update) | async-done | bytes 524304 | tf_op jit(solution)/shard_map/reduce_scatter | solution.py:302
  891.0 430.5 %all-reduce.5 = (f32[256]{0:T(256)}, f32[256,256]{1,0:T(8,128)}, f32[256,256]{1,0:T(8,128)}, f32[256,1024]{1,0:T(8,128)}, f32[256,1024]{1,0:T(8,128)}, /*index=5...) all-reduce(f32[256]{0:T(256)S(1)} %get-tuple-element.267, ...), channel_id=1, replica_groups=mesh['ctx'=8,'fsdp'=4] {'ctx'}, use_global_device_ids=true, to_apply=%region_13.14 | all-reduce | flops 2769408 | bytes 16617472 | tf_op jit(solution)/shard_map/psum | solution.py:321
  (312 shorter events, 194.6 us)
Async XLA Ops:
  7.2 28.8 %all-gather.11.cloned.1.call-start = ((), (), s32[]{:S(2)}) async-start(), calls=%async_computation.8 | async-start | bytes 2621440 | tf_op jit(solution)/shard_map/all_gather | solution.py:71
  7.9 28.1 %copy-start.10 = (bf16[1,512,1024]{2,1,0:T(8,128)(2,1)S(1)}, bf16[1,512,1024]{2,1,0:T(8,128)(2,1)}, u32[]{:S(2)}) copy-start(bf16[1,512,1024]{2,1,0:T(8,128)(2,1)} %param.16) | copy-start | bytes 3145732
  7.9 158.1 %all-gather.13.cloned.1.call-start = ((), (), s32[]{:S(2)}) async-start(), calls=%async_computation.9 | async-start | bytes 2359296 | tf_op jit(solution)/shard_map/all_gather | solution.py:116
  14.7 42.7 %copy-start.53 = (f32[4,1,256]{2,1,0:T(1,128)}, f32[4,1,256]{2,1,0:T(1,128)S(1)}, u32[]{:S(2)}) copy-start(f32[4,1,256]{2,1,0:T(1,128)S(1)} %convert_element_type.281) | copy-start | bytes 12292
  26.3 31.2 %copy-start.58 = (f32[512]{0:T(512)}, f32[512]{0:T(512)S(1)}, u32[]{:S(2)}) copy-start(f32[512]{0:T(512)S(1)} %get-tuple-element.253) | copy-start | bytes 6148
  28.9 389.7 %all-gather.15.cloned.1.call-start = ((), (), s32[]{:S(2)}) async-start(), calls=%async_computation.10 | async-start | bytes 2621440 | tf_op jit(solution)/shard_map/all_gather | solution.py:72
  29.6 395.0 %all-gather.17.cloned.1.call-start = ((), (), s32[]{:S(2)}) async-start(), calls=%async_computation.11 | async-start | bytes 7045120 | tf_op jit(solution)/shard_map/all_gather | solution.py:74
  30.2 402.9 %all-gather.19.cloned.1.call-start = ((), (), s32[]{:S(2)}) async-start(), calls=%async_computation.12 | async-start | bytes 7045120 | tf_op jit(solution)/shard_map/all_gather | solution.py:75
  43.5 213.5 %all-to-all-start = ((bf16[8,512,1024]{1,2,0:T(8,128)(2,1)}), bf16[8,512,1024]{1,2,0:T(8,128)(2,1)}, u32[]{:S(2)}, u32[]{:S(2)}) async-start(bf16[8,512,1024]{1,2,0:T(8,128)(2,1)} %stack.2), calls=%async_computation | async-start | bytes 16777216 | tf_op jit(solution)/shard_map/all_to_all | solution.py:118
  49.6 9.9 copy-start.39
  49.6 14.2 %copy-start.67 = (s32[1,16]{1,0:T(1,128)S(1)}, s32[1,16]{1,0:T(1,128)}, u32[]{:S(2)}) copy-start(s32[1,16]{1,0:T(1,128)} %param.17) | copy-start | bytes 196
  49.6 15.0 %copy-start.66 = (bf16[256]{0:T(256)(128)(2,1)S(1)}, bf16[256]{0:T(256)(128)(2,1)}, u32[]{:S(2)}) copy-start(bf16[256]{0:T(256)(128)(2,1)} %param.23) | copy-start | bytes 1540
  49.6 392.1 %all-gather.21.cloned.1.call-start = ((), (), s32[]{:S(2)}) async-start(), calls=%async_computation.13 | async-start | bytes 7045120 | tf_op jit(solution)/shard_map/all_gather | solution.py:76
  50.2 507.1 %all-gather.23.cloned.1.call-start = ((), (), s32[]{:S(2)}) async-start(), calls=%async_computation.14 | async-start | bytes 2359296 | tf_op jit(solution)/shard_map/all_gather | solution.py:218
  59.4 546.1 %all-gather.25.cloned.1.call-start = ((), (), s32[]{:S(2)}) async-start(), calls=%async_computation.15 | async-start | bytes 9437184 | tf_op jit(solution)/shard_map/all_gather | solution.py:219
  63.2 18.1 %copy-start.28 = (bf16[2,256,16,16]{1,0,3,2:T(2,128)(2,1)}, bf16[2,256,16,16]{1,0,3,2:T(2,128)(2,1)S(1)}, u32[]{:S(2)}) copy-start(bf16[2,256,16,16]{1,0,3,2:T(2,128)(2,1)S(1)} %reshape.240) | copy-start | bytes 786436
  281.6 122.0 %copy-start.44 = (bf16[2,256,16,16]{1,3,2,0:T(8,128)(2,1)S(1)}, bf16[2,256,16,16]{1,3,2,0:T(8,128)(2,1)}, u32[]{:S(2)}) copy-start(bf16[2,256,16,16]{1,3,2,0:T(8,128)(2,1)} %get-tuple-element.250) | copy-start | bytes 786436
  281.6 122.0 %copy-start.64 = (bf16[273]{0:T(512)(128)(2,1)S(1)}, bf16[273]{0:T(512)(128)(2,1)}, u32[]{:S(2)}) copy-start(bf16[273]{0:T(512)(128)(2,1)} %pad.9.clone) | copy-start | bytes 1642
  283.1 10.2 slice-start
  284.4 8.9 slice-start.1
  311.5 19.4 %copy-start = (bf16[8,256,16,16]{1,3,2,0:T(8,128)(2,1)S(1)}, bf16[8,256,16,16]{1,3,2,0:T(8,128)(2,1)}, u32[]{:S(2)}) copy-start(bf16[8,256,16,16]{1,3,2,0:T(8,128)(2,1)} %get-tuple-element.357) | copy-start | bytes 3145732 | tf_op jit(solution)/shard_map/while
  344.4 10.2 slice-start
  345.8 8.9 slice-start.1
  371.6 19.4 %copy-start = (bf16[8,256,16,16]{1,3,2,0:T(8,128)(2,1)S(1)}, bf16[8,256,16,16]{1,3,2,0:T(8,128)(2,1)}, u32[]{:S(2)}) copy-start(bf16[8,256,16,16]{1,3,2,0:T(8,128)(2,1)} %get-tuple-element.357) | copy-start | bytes 3145732 | tf_op jit(solution)/shard_map/while
  403.6 9.6 slice-start.2
  422.8 10.4 copy-start.56
  479.4 345.5 %reduce-scatter.8.cloned.1.call-start = ((), (), s32[]{:S(2)}) async-start(), calls=%async_computation.16 | async-start | bytes 655360 | tf_op jit(solution)/shard_map/reduce_scatter | solution.py:296
  491.6 29.7 %copy-start.9 = (bf16[2,256,16,64]{1,3,2,0:T(8,128)(2,1)}, bf16[2,256,16,64]{1,3,2,0:T(8,128)(2,1)S(1)}, u32[]{:S(2)}) copy-start(bf16[2,256,16,64]{1,3,2,0:T(8,128)(2,1)S(1)} %get-tuple-element.246) | copy-start | bytes 3145732
  504.9 16.5 %copy-start.15 = (bf16[2,256,16,64]{1,0,3,2:T(2,128)(2,1)S(1)}, bf16[2,256,16,64]{1,0,3,2:T(2,128)(2,1)}, u32[]{:S(2)}) copy-start(bf16[2,256,16,64]{1,0,3,2:T(2,128)(2,1)} %reshape.239) | copy-start | bytes 3145732
  521.3 7.8 copy-start.31
  533.8 291.2 %reduce-scatter.14.cloned.1.call-start = ((), (), s32[]{:S(2)}) async-start(), calls=%async_computation.19 | async-start | bytes 2621440 | tf_op jit(solution)/shard_map/reduce_scatter | solution.py:305
  536.5 288.5 %reduce-scatter.16.cloned.1.call-start = ((), (), s32[]{:S(2)}) async-start(), calls=%async_computation.20 | async-start | bytes 7045120 | tf_op jit(solution)/shard_map/reduce_scatter | solution.py:311
  544.2 280.8 %reduce-scatter.18.cloned.1.call-start = ((), (), s32[]{:S(2)}) async-start(), calls=%async_computation.21 | async-start | bytes 7045120 | tf_op jit(solution)/shard_map/reduce_scatter | solution.py:314
  552.2 279.6 %reduce-scatter.20.cloned.1.call-start = ((), (), s32[]{:S(2)}) async-start(), calls=%async_computation.22 | async-start | bytes 7045120 | tf_op jit(solution)/shard_map/reduce_scatter | solution.py:317
  561.3 35.1 %copy-start.37 = (bf16[1,512,1024]{2,1,0:T(8,128)(2,1)S(1)}, bf16[1,512,1024]{2,1,0:T(8,128)(2,1)}, u32[]{:S(2)}) copy-start(bf16[1,512,1024]{2,1,0:T(8,128)(2,1)} %param.27) | copy-start | bytes 3145732
  561.3 35.1 %copy-start.71 = (bf16[512,2752]{0,1:T(8,128)(2,1)S(1)}, bf16[512,2752]{0,1:T(8,128)(2,1)}, u32[]{:S(2)}) copy-start(bf16[512,2752]{0,1:T(8,128)(2,1)} %get-tuple-element.245) | copy-start | bytes 8454148
  601.4 255.2 %reduce-scatter.10.cloned.1.call-start = ((), (), s32[]{:S(2)}) async-start(), calls=%async_computation.17 | async-start | bytes 655360 | tf_op jit(solution)/shard_map/reduce_scatter | solution.py:299
  627.7 19.7 %copy-start.46 = (s32[2]{0:T(128)S(1)}, s32[2]{0:T(128)}, u32[]{:S(2)}) copy-start(s32[2]{0:T(128)} %copy-done.45) | copy-start | bytes 28
  627.7 19.7 %copy-start.69 = (s32[2,8]{1,0:T(2,128)S(1)}, s32[2,8]{1,0:T(2,128)}, u32[]{:S(2)}) copy-start(s32[2,8]{1,0:T(2,128)} %copy-done.68) | copy-start | bytes 196
  672.4 20.6 %copy-start.8 = (bf16[8,256,16,16]{1,3,2,0:T(8,128)(2,1)S(1)}, bf16[8,256,16,16]{1,3,2,0:T(8,128)(2,1)}, u32[]{:S(2)}) copy-start(bf16[8,256,16,16]{1,3,2,0:T(8,128)(2,1)} %get-tuple-element.367) | copy-start | bytes 3145732 | tf_op jit(solution)/shard_map/while
  727.8 20.8 %copy-start.8 = (bf16[8,256,16,16]{1,3,2,0:T(8,128)(2,1)S(1)}, bf16[8,256,16,16]{1,3,2,0:T(8,128)(2,1)}, u32[]{:S(2)}) copy-start(bf16[8,256,16,16]{1,3,2,0:T(8,128)(2,1)} %get-tuple-element.367) | copy-start | bytes 3145732 | tf_op jit(solution)/shard_map/while
  771.5 17.3 %copy-start.2 = (bf16[2,16,256,256]{2,3,1,0:T(8,128)(2,1)S(1)}, bf16[2,16,256,256]{2,3,1,0:T(8,128)(2,1)}, u32[]{:S(2)}) copy-start(bf16[2,16,256,256]{2,3,1,0:T(8,128)(2,1)} %copy-done.1) | copy-start | bytes 12582916
  771.5 17.3 %copy-start.29 = (bf16[2,256,16,16]{1,0,3,2:T(2,128)(2,1)S(1)}, bf16[2,256,16,16]{1,0,3,2:T(2,128)(2,1)}, u32[]{:S(2)}) copy-start(bf16[2,256,16,16]{1,0,3,2:T(2,128)(2,1)} %copy-done.28) | copy-start | bytes 786436
  802.0 89.0 %reduce-scatter.12.cloned.1.call-start = ((), (), s32[]{:S(2)}) async-start(), calls=%async_computation.18 | async-start | bytes 2621440 | tf_op jit(solution)/shard_map/reduce_scatter | solution.py:302
  825.0 10.1 copy-start.43
  835.1 10.2 copy-start.19
  835.1 10.2 copy-start.61
  839.2 51.7 %copy-start.48 = (bf16[256,256]{1,0:T(8,128)(2,1)S(1)}, bf16[256,256]{1,0:T(8,128)(2,1)}, u32[]{:S(2)}) copy-start(bf16[256,256]{1,0:T(8,128)(2,1)} %reduce-scatter.8.cloned.1.call-done) | copy-start | bytes 393220
  (48 other events, 196.1 us)
Sparse Core Ops, SparseCore 0:
  9.6 26.3 all-gather.10
  38.7 127.2 all-gather.12
  167.6 32.2 all-gather.14
  201.3 43.3 all-gather.16
  246.1 43.3 all-gather.18
  291.0 42.6 all-gather.20
  335.8 49.2 all-gather.22
  479.6 125.8 all-gather.24
  608.0 19.9 reduce-scatter.7
  630.5 31.4 reduce-scatter.13
  664.5 53.9 reduce-scatter.15
  721.2 54.0 reduce-scatter.17
  777.8 54.0 reduce-scatter.19
  834.9 21.6 reduce-scatter.9
  859.5 31.4 reduce-scatter.11
